TPU v7x, 512 devices: a whole 4x8x8 slice. The times are simulated.
512 devices in a mesh: seq: 64 (over x, y, core), head: 8 (over z).
Axes of the slice: x: 4, y: 8, z: 8, core: 2. Of those that a mesh axis runs over, the one named last changes fastest.
Arguments:
- text_rows: bfloat16 [8192, 4096], P('seq', 'head'), may hold values from -6 to 6
- picture_rows: bfloat16 [2048, 4096], P('seq', 'head'), may hold values from -6 to 6
- picture_slots: int32 [2048], P('seq'), may hold values from 0 to 8191, as said below
- norm_gain: float32 [4096], replicated, may hold values from 0.1 to 1.9
- w_query: bfloat16 [4096, 4096], P('seq', 'head'), may hold values from -1 to 1
- w_key: bfloat16 [4096, 1024], P('seq', 'head'), may hold values from -1 to 1
- w_value: bfloat16 [4096, 1024], P('seq', 'head'), may hold values from -0.09375 to 0.09375
- w_out: bfloat16 [4096, 4096], P('head', 'seq'), may hold values from -0.5 to 0.5
- cache_keys: bfloat16 [4096, 1024], P('seq', 'head'), may hold values from -500 to 500
- cache_values: bfloat16 [4096, 1024], P('seq', 'head'), may hold values from -6 to 6
- recompute_rows: bfloat16 [512, 4096], P('seq', 'head'), may hold values from -6 to 6
- recompute_slots: int32 [512], P('seq'), may hold values from 0 to 4095, as said below
Outputs:
- mixed: bfloat16 [8192, 4096], P('seq', 'head')
Inputs may be any that keep to these rules, and one draw needn't show every extreme that they name: `picture_slots`: distinct stream positions, in runs of 256 consecutive positions, one run a tile; the first tile's run starts at position 4096 and the last tile's run ends at the stream's last position. `recompute_slots`: each aligned block b of 8 entries names distinct rows of cache rows b * 64 to (b + 1) * 64 - 1.
All inputs are finite; a program needn't handle non-finite values.
Results may differ from a plain program's by a relative error of at most 0.02.
Values may be sent and summed in bfloat16 or wider, within the bound.
A program may use at most 128 MiB of HBM per device.

v0:
```python
import jax
import jax.numpy as jnp
from jax import lax
from jax.sharding import PartitionSpec as P

D = 4096
HD = 128
EPSILON = 1e-05
ROPE_BASE = 1000000.0
NEG_FILL = -1e30


def rotate(values, positions):
    half = values.shape[-1] // 2
    freqs = ROPE_BASE ** (-jnp.arange(half, dtype=jnp.float32) / half)
    angles = positions[:, None] * freqs[None, :]
    cosine = jnp.cos(angles)[:, None, :]
    sine = jnp.sin(angles)[:, None, :]
    first = values[..., :half]
    second = values[..., half:]
    return jnp.concatenate(
        [first * cosine - second * sine, second * cosine + first * sine], axis=-1
    )


def scaled(rows_wide, squares, gain):
    return (rows_wide * lax.rsqrt(squares / D + EPSILON)[:, None] * gain[None, :]).astype(
        jnp.bfloat16
    )


def attend(carry, key_piece, value_piece, queries, allowed):
    best, total, accum = carry
    count = key_piece.shape[0]
    kv_local = queries.shape[0]
    keys_split = key_piece.reshape(count, kv_local, HD)
    values_split = value_piece.reshape(count, kv_local, HD)
    scores = jnp.einsum(
        "kgtd,nkd->kgtn", queries, keys_split, preferred_element_type=jnp.float32
    ) * HD ** (-0.5)
    scores = jnp.where(allowed, scores, NEG_FILL)
    fresh = jnp.maximum(best, jnp.max(scores, axis=-1))
    factor = jnp.exp(best - fresh)
    weights = jnp.where(allowed, jnp.exp(scores - fresh[..., None]), 0.0)
    total = total * factor + jnp.sum(weights, axis=-1)
    accum = accum * factor[..., None] + jnp.einsum(
        "kgtn,nkd->kgtd",
        weights.astype(jnp.bfloat16),
        values_split,
        preferred_element_type=jnp.float32,
    )
    return (fresh, total, accum)


def on_device(
    text_rows,
    picture_rows,
    picture_slots,
    norm_gain,
    w_query,
    w_key,
    w_value,
    w_out,
    cache_keys,
    cache_values,
    recompute_rows,
    recompute_slots,
):
    tok_rows = text_rows.shape[0]
    rec_count = recompute_rows.shape[0]
    cache_rows = cache_keys.shape[0]
    seq_index = lax.axis_index("seq")
    local_pos = seq_index * tok_rows + jnp.arange(tok_rows, dtype=jnp.int32)
    rows_piece = lax.all_gather(picture_rows, "seq", axis=0, tiled=True)
    slots_piece = lax.all_gather(picture_slots, "seq", axis=0, tiled=True)
    select = (slots_piece[None, :] == local_pos[:, None]).astype(jnp.bfloat16)
    placed = jnp.dot(select, rows_piece, preferred_element_type=jnp.float32)
    hits = jnp.sum(select.astype(jnp.float32), axis=1)
    added, hits = (placed, hits)
    stream = jnp.where(hits[:, None] > 0.5, added, text_rows.astype(jnp.float32)).astype(
        jnp.bfloat16
    )
    slice_width = stream.shape[1]
    gain_slice = lax.dynamic_slice_in_dim(
        norm_gain, lax.axis_index("head") * slice_width, slice_width, 0
    )
    stream_wide = stream.astype(jnp.float32)
    rec_wide = recompute_rows.astype(jnp.float32)
    stream_sq, rec_sq = lax.psum(
        (jnp.sum(stream_wide * stream_wide, axis=1), jnp.sum(rec_wide * rec_wide, axis=1)), "head"
    )
    normed, rec_normed = (
        lax.all_gather(scaled(stream_wide, stream_sq, gain_slice), "head", axis=1, tiled=True),
        lax.all_gather(scaled(rec_wide, rec_sq, gain_slice), "head", axis=1, tiled=True),
    )
    stacked = jnp.concatenate([normed, rec_normed], axis=0)
    query_cols = w_query.shape[1]
    key_cols = w_key.shape[1]
    pieces = (
        lax.all_gather(w_query, "seq", axis=0, tiled=True),
        lax.all_gather(w_key, "seq", axis=0, tiled=True),
        lax.all_gather(w_value, "seq", axis=0, tiled=True),
    )
    query_all = jnp.dot(stacked, pieces[0], preferred_element_type=jnp.float32)
    key_all = jnp.dot(stacked, pieces[1], preferred_element_type=jnp.float32)
    value_all = jnp.dot(stacked, pieces[2], preferred_element_type=jnp.float32)
    cache_total = cache_rows * lax.axis_size("seq")
    stream_pos = (cache_total + local_pos).astype(jnp.float32)
    rec_pos = recompute_slots.astype(jnp.float32)
    heads_local = query_cols // HD
    kv_local = key_cols // HD
    group = heads_local // kv_local
    rot_query = rotate(query_all[:tok_rows].reshape(tok_rows, heads_local, HD), stream_pos).astype(
        jnp.bfloat16
    )
    rot_key = (
        rotate(key_all[:tok_rows].reshape(tok_rows, kv_local, HD), stream_pos)
        .astype(jnp.bfloat16)
        .reshape(tok_rows, key_cols)
    )
    values_new = value_all[:tok_rows].astype(jnp.bfloat16)
    rot_rec_key = (
        rotate(key_all[tok_rows:].reshape(rec_count, kv_local, HD), rec_pos)
        .astype(jnp.bfloat16)
        .reshape(rec_count, key_cols)
    )
    rec_values = value_all[tok_rows:].astype(jnp.bfloat16)
    local_slots = recompute_slots - seq_index * cache_rows
    select = local_slots[:, None] == jnp.arange(cache_rows, dtype=jnp.int32)[None, :]
    replaced = jnp.any(select, axis=0)[:, None]
    select_cols = select.astype(jnp.bfloat16).T
    new_keys = jnp.dot(select_cols, rot_rec_key, preferred_element_type=jnp.float32).astype(
        jnp.bfloat16
    )
    new_values = jnp.dot(select_cols, rec_values, preferred_element_type=jnp.float32).astype(
        jnp.bfloat16
    )
    cache_k = jnp.where(replaced, new_keys, cache_keys)
    cache_v = jnp.where(replaced, new_values, cache_values)
    queries = jnp.transpose(rot_query.reshape(tok_rows, kv_local, group, HD), (1, 2, 0, 3))
    carry_start = (
        jnp.full((kv_local, group, tok_rows), NEG_FILL, jnp.float32),
        jnp.zeros((kv_local, group, tok_rows), jnp.float32),
        jnp.zeros((kv_local, group, tok_rows, HD), jnp.float32),
    )
    pieces = (
        lax.all_gather(cache_k, "seq", axis=0, tiled=True),
        lax.all_gather(cache_v, "seq", axis=0, tiled=True),
    )
    allowed = jnp.ones((tok_rows, pieces[0].shape[0]), jnp.bool_)
    carry_mid = attend(carry_start, pieces[0], pieces[1], queries, allowed)
    pieces = (
        lax.all_gather(rot_key, "seq", axis=0, tiled=True),
        lax.all_gather(values_new, "seq", axis=0, tiled=True),
    )
    key_pos = jnp.arange(pieces[0].shape[0], dtype=jnp.int32)
    allowed = key_pos[None, :] <= local_pos[:, None]
    best, total, accum = attend(carry_mid, pieces[0], pieces[1], queries, allowed)
    attended = (
        jnp.transpose(accum / total[..., None], (2, 0, 1, 3))
        .reshape(tok_rows, query_cols)
        .astype(jnp.bfloat16)
    )
    partial_out = jnp.dot(
        attended,
        lax.all_gather(w_out, "seq", axis=1, tiled=True),
        preferred_element_type=jnp.float32,
    )
    return lax.psum_scatter(
        partial_out.astype(jnp.bfloat16), "head", scatter_dimension=1, tiled=True
    )


def solution(mesh):
    return jax.shard_map(
        on_device,
        mesh=mesh,
        in_specs=(
            P("seq", "head"),
            P("seq", "head"),
            P("seq"),
            P(),
            P("seq", "head"),
            P("seq", "head"),
            P("seq", "head"),
            P("head", "seq"),
            P("seq", "head"),
            P("seq", "head"),
            P("seq", "head"),
            P("seq"),
        ),
        out_specs=P("seq", "head"),
        check_vma=False,
    )
```

profile of v0, /device:TPU:2, one launch (start us, length us, event | category | flops | bytes accessed | tf_op | source)
XLA Modules:
  0.0 877.7 jit_solution(5738790809692181335)
XLA Ops:
  6.5 0.7 all-gather.11.cloned.1.call-update
  7.3 0.0 all-gather.13.cloned.1.call-start
  7.3 1.3 dynamic-slice
  9.2 0.8 dynamic_slice.3
  10.0 0.8 dynamic-update-slice
  10.8 20.5 %all-reduce = s32[2048]{0:T(1024)S(1)} all-reduce(s32[2048]{0:T(1024)S(1)} %dynamic-update-slice), channel_id=1, replica_groups=mesh['seq'=64,'head'=8] {'seq'}, use_global_device_ids=true, to_apply=%add | all-reduce | flops 2048 | bytes 16384
  31.4 0.8 fusion.60
  32.2 0.3 convert_reduce_fusion
  32.5 64.4 %all-gather.11.cloned.1.call-done = bf16[2048,512]{1,0:T(8,128)(2,1)} async-done(((bf16[32,512]{1,0:T(8,128)(2,1)}), bf16[2048,512]{1,0:T(8,128)(2,1)}) %all-gather.11.cloned.1.call-update) | async-done | bytes 2097168 | tf_op jit(solution)/shard_map/all_gather | solution.py:74
  96.8 2.2 multiply_reduce_fusion.1
  99.0 18.1 %all-reduce.1 = (f32[128]{0:T(128)S(1)}, f32[8]{0:T(128)S(1)}) all-reduce(f32[128]{0:T(128)S(1)} %get-tuple-element.24, f32[8]{0:T(128)S(1)} %fusion.60), channel_id=1, replica_groups=mesh['seq'=64,'head'=8] {'head'}, use_global_device_ids=true, to_apply=%region_2.3 | all-reduce | flops 136 | bytes 1088 | tf_op jit(solution)/shard_map/psum | solution.py:89
  117.1 0.8 multiply_convert_fusion
  117.9 0.0 all-gather.17.cloned.1.call-start
  117.9 0.7 all-gather.17.cloned.1.call-update
  118.6 0.0 all-gather.21.cloned.1.call-start
  118.7 0.5 all-gather.21.cloned.1.call-update
  119.2 0.0 all-gather.15.cloned.1.call-start
  119.2 0.5 all-gather.15.cloned.1.call-update
  119.8 0.0 all-gather.19.cloned.1.call-start
  119.9 0.7 fusion.89
  120.6 0.1 fusion.71
  120.7 0.8 fusion.62
  121.5 24.6 %all_gather.39 = bf16[8,4096]{1,0:T(8,128)(2,1)S(1)} all-gather(bf16[8,512]{1,0:T(8,128)(2,1)S(1)} %fusion.62), channel_id=1, replica_groups=mesh['seq'=64,'head'=8] {'head'}, dimensions={1}, use_global_device_ids=true | all-gather | bytes 73728 | tf_op jit(solution)/shard_map/all_gather | solution.py:94
  146.0 10.3 %all-gather.13.cloned.1.call-done = bf16[128,4096]{1,0:T(8,128)(2,1)} async-done(((bf16[128,512]{1,0:T(8,128)(2,1)}), bf16[128,4096]{1,0:T(8,128)(2,1)}) %all-gather.13.cloned.1.call-update) | async-done | bytes 1048592 | tf_op jit(solution)/shard_map/all_gather | solution.py:93
  156.3 1.3 constant_dynamic-update-slice_fusion.1
  157.6 80.6 %all-gather.17.cloned.1.call-done = bf16[4096,128]{1,0:T(8,128)(2,1)} async-done(((bf16[64,128]{1,0:T(8,128)(2,1)}), bf16[4096,128]{1,0:T(8,128)(2,1)}) %all-gather.17.cloned.1.call-update) | async-done | bytes 1048592 | tf_op jit(solution)/shard_map/all_gather | solution.py:101
  238.2 1.7 fusion.90
  239.9 0.1 fusion.79
  240.0 1.6 fusion.33
  241.6 0.0 all-gather.19.cloned.1.call-update
  241.6 0.0 all-gather.25.cloned.1.call-start
  241.7 0.3 fusion.59
  242.0 0.7 pad_maximum_fusion
  242.7 0.0 all-gather.25.cloned.1.call-update
  242.7 0.0 all-gather.27.cloned.1.call-start
  242.8 78.3 %all-gather.21.cloned.1.call-done = bf16[4096,128]{1,0:T(8,128)(2,1)} async-done(((bf16[64,128]{1,0:T(8,128)(2,1)}), bf16[4096,128]{1,0:T(8,128)(2,1)}) %all-gather.21.cloned.1.call-update) | async-done | bytes 1048592 | tf_op jit(solution)/shard_map/all_gather | solution.py:102
  321.1 1.7 convolution_convert_fusion.1
  322.7 0.6 slice.55
  323.3 0.0 all-gather.27.cloned.1.call-update
  323.4 0.0 all-gather.23.cloned.1.call-start
  323.4 0.9 fusion.34
  324.3 0.0 all-gather.29.cloned.1.call-start
  324.4 0.5 all-gather.29.cloned.1.call-update
  324.9 0.0 reduce-scatter.2.cloned.1.call-start
  325.0 0.3 multiply_cosine_fusion.1
  325.3 0.7 iota_compare_fusion
  325.9 80.4 %all-gather.15.cloned.1.call-done = bf16[4096,512]{1,0:T(8,128)(2,1)} async-done(((bf16[64,512]{1,0:T(8,128)(2,1)}), bf16[4096,512]{1,0:T(8,128)(2,1)}) %all-gather.15.cloned.1.call-update) | async-done | bytes 4194320 | tf_op jit(solution)/shard_map/all_gather | solution.py:100
  406.3 2.9 fusion.41
  409.2 0.1 reshape.377
  409.3 0.2 fusion.88
  409.5 0.1 fusion.48
  409.6 79.5 %all-gather.19.cloned.1.call-done = bf16[4096,128]{1,0:T(8,128)(2,1)} async-done(((bf16[64,128]{1,0:T(8,128)(2,1)}), bf16[4096,128]{1,0:T(8,128)(2,1)}) %all-gather.19.cloned.1.call-update) | async-done | bytes 1048592 | tf_op jit(solution)/shard_map/all_gather | solution.py:147
  489.1 5.7 multiply_reduce_fusion
  494.8 78.2 %all-gather.25.cloned.1.call-done = bf16[8192,128]{1,0:T(8,128)(2,1)} async-done(((bf16[128,128]{1,0:T(8,128)(2,1)}), bf16[8192,128]{1,0:T(8,128)(2,1)}) %all-gather.25.cloned.1.call-update) | async-done | bytes 2097168 | tf_op jit(solution)/shard_map/all_gather | solution.py:153
  573.0 5.0 fusion
  578.0 1.5 fusion.6
  579.5 5.0 fusion.1
  584.5 72.4 %all-gather.27.cloned.1.call-done = bf16[8192,128]{1,0:T(8,128)(2,1)} async-done(((bf16[128,128]{1,0:T(8,128)(2,1)}), bf16[8192,128]{1,0:T(8,128)(2,1)}) %all-gather.27.cloned.1.call-update) | async-done | bytes 2097168 | tf_op jit(solution)/shard_map/all_gather | solution.py:154
  656.9 9.9 %fusion.3 = f32[4,128,128]{1,2,0:T(8,128)S(1)} fusion(f32[4,128,8192]{2,1,0:T(8,128)} %copy-done, f32[4,128]{1,0:T(4,128)S(1)} %get-tuple-element.18, pred[128,8192]{1,0:T(8,128)(4,1)S(1)} %iota_compare_fusion, bf16[8192,128]{1,0:T(8,128)(2,1)} %all-gather.27.cloned.1.call-done), kind=kOutput, calls=%fused_computation.6 | convolution fusion | flops 1094713344 | bytes 20187136 | tf_op jit(solution)/shard_map/kgtn,nkd->kgtd/dot_general | solution.py:46
  666.8 73.1 %all-gather.23.cloned.1.call-done = bf16[4096,128]{1,0:T(8,128)(2,1)} async-done(((bf16[64,128]{1,0:T(8,128)(2,1)}), bf16[4096,128]{1,0:T(8,128)(2,1)}) %all-gather.23.cloned.1.call-update) | async-done | bytes 1048592 | tf_op jit(solution)/shard_map/all_gather | solution.py:148
  740.0 5.4 fusion.38
  745.4 79.8 %all-gather.29.cloned.1.call-done = bf16[512,4096]{0,1:T(8,128)(2,1)} async-done(((bf16[512,64]{0,1:T(8,128)(2,1)}), bf16[512,4096]{0,1:T(8,128)(2,1)}) %all-gather.29.cloned.1.call-update) | async-done | bytes 4194320 | tf_op jit(solution)/shard_map/all_gather | solution.py:166
  825.2 4.7 convolution_convert_fusion
  829.9 41.3 %reduce-scatter.2.cloned.1.call-done = bf16[128,512]{1,0:T(8,128)(2,1)} async-done(((bf16[128,4096]{1,0:T(8,128)(2,1)}), bf16[128,512]{1,0:T(8,128)(2,1)}) %reduce-scatter.2.cloned.1.call-update) | async-done | bytes 131088 | tf_op jit(solution)/shard_map/reduce_scatter | solution.py:169
  (22 shorter events, 0.1 us)
Async XLA Ops:
  6.5 316.9 %copy-start.2 = (bf16[64,128]{1,0:T(8,128)(2,1)S(1)}, bf16[64,128]{1,0:T(8,128)(2,1)}, u32[]{:S(2)}) copy-start(bf16[64,128]{1,0:T(8,128)(2,1)} %param.21) | copy-start | bytes 49156
  6.5 90.3 %all-gather.11.cloned.1.call-start = ((), (), s32[]{:S(2)}) async-start(), calls=%async_computation.1 | async-start | bytes 2129920 | tf_op jit(solution)/shard_map/all_gather | solution.py:74
  7.3 149.1 %all-gather.13.cloned.1.call-start = ((), (), s32[]{:S(2)}) async-start(), calls=%async_computation.2 | async-start | bytes 1179648 | tf_op jit(solution)/shard_map/all_gather | solution.py:93
  117.9 120.3 %all-gather.17.cloned.1.call-start = ((), (), s32[]{:S(2)}) async-start(), calls=%async_computation.4 | async-start | bytes 1064960 | tf_op jit(solution)/shard_map/all_gather | solution.py:101
  118.6 202.4 %all-gather.21.cloned.1.call-start = ((), (), s32[]{:S(2)}) async-start(), calls=%async_computation.6 | async-start | bytes 1064960 | tf_op jit(solution)/shard_map/all_gather | solution.py:102
  119.2 287.1 %all-gather.15.cloned.1.call-start = ((), (), s32[]{:S(2)}) async-start(), calls=%async_computation.3 | async-start | bytes 4259840 | tf_op jit(solution)/shard_map/all_gather | solution.py:100
  119.8 369.3 %all-gather.19.cloned.1.call-start = ((), (), s32[]{:S(2)}) async-start(), calls=%async_computation.5 | async-start | bytes 1064960 | tf_op jit(solution)/shard_map/all_gather | solution.py:147
  241.6 331.4 %all-gather.25.cloned.1.call-start = ((), (), s32[]{:S(2)}) async-start(), calls=%async_computation.8 | async-start | bytes 2129920 | tf_op jit(solution)/shard_map/all_gather | solution.py:153
  242.7 414.2 %all-gather.27.cloned.1.call-start = ((), (), s32[]{:S(2)}) async-start(), calls=%async_computation.9 | async-start | bytes 2129920 | tf_op jit(solution)/shard_map/all_gather | solution.py:154
  323.4 416.6 %all-gather.23.cloned.1.call-start = ((), (), s32[]{:S(2)}) async-start(), calls=%async_computation.7 | async-start | bytes 1064960 | tf_op jit(solution)/shard_map/all_gather | solution.py:148
  324.3 500.9 %all-gather.29.cloned.1.call-start = ((), (), s32[]{:S(2)}) async-start(), calls=%async_computation.10 | async-start | bytes 4259840 | tf_op jit(solution)/shard_map/all_gather | solution.py:166
  324.9 546.2 %reduce-scatter.2.cloned.1.call-start = ((), (), s32[]{:S(2)}) async-start(), calls=%async_computation.11 | async-start | bytes 1179648 | tf_op jit(solution)/shard_map/reduce_scatter | solution.py:169
  573.0 5.0 copy-start.1
  578.0 6.5 copy-start
Sparse Core Ops, SparseCore 0:
  10.7 86.0 all-gather.10
  118.0 38.2 all-gather.12
  159.7 78.4 all-gather.16
  241.4 79.6 all-gather.20
  324.3 82.0 all-gather.14
  409.5 79.4 all-gather.18
  492.4 80.5 all-gather.24
  576.4 80.5 all-gather.26
  660.3 79.6 all-gather.22
  743.2 82.0 all-gather.28
  830.0 41.0 reduce-scatter.1
where the time goes:
time: 878 us
  waiting for transfers between devices  741 us (84%)
  blocking collectives  63.2 us (7%)
  matrix products  41.5 us (5%)
  between operations  14.1 us (2%)
  other arithmetic  12.1 us (1%)
    all_gather x1, waiting for transfers between devices, on_device(): lax.all_gather(w_key, 'seq', axis=0, tiled=True)  80.6 us
    all_gather x1, waiting for transfers between devices, on_device(): lax.all_gather(w_query, 'seq', axis=0, tiled=True)  80.4 us
    all_gather x1, waiting for transfers between devices, on_device(): lax.all_gather(w_out, 'seq', axis=1, tiled=True)  79.8 us
    all_gather x1, waiting for transfers between devices, on_device(): lax.all_gather(cache_k, 'seq', axis=0, tiled=True)  79.5 us
    all_gather x1, waiting for transfers between devices, on_device(): lax.all_gather(w_value, 'seq', axis=0, tiled=True)  78.3 us
    all_gather x1, waiting for transfers between devices, on_device(): lax.all_gather(rot_key, 'seq', axis=0, tiled=True)  78.2 us
    all_gather x1, waiting for transfers between devices, on_device(): lax.all_gather(cache_v, 'seq', axis=0, tiled=True)  73.1 us
    all_gather x1, waiting for transfers between devices, on_device(): lax.all_gather(values_new, 'seq', axis=0, tiled=True)  72.4 us
  transfers between devices with their start and end apart: 11, of which 11 were waited for; matrix products, arithmetic and copies ran while one was open for 6% of the time, Pallas kernels for 0%

commit v1 on v0

--- a/solution.py
+++ b/solution.py
@@ -8,6 +8,11 @@
 EPSILON = 1e-05
 ROPE_BASE = 1000000.0
 NEG_FILL = -1e30
+
+
+def gather_by_exchange(shard, axis, dim):
+    copies = jnp.concatenate([shard] * lax.axis_size(axis), axis=dim)
+    return lax.all_to_all(copies, axis, dim, dim, tiled=True)
 
 
 def rotate(values, positions):
@@ -99,7 +104,7 @@
     pieces = (
         lax.all_gather(w_query, "seq", axis=0, tiled=True),
         lax.all_gather(w_key, "seq", axis=0, tiled=True),
-        lax.all_gather(w_value, "seq", axis=0, tiled=True),
+        gather_by_exchange(w_value, "seq", 0),
     )
     query_all = jnp.dot(stacked, pieces[0], preferred_element_type=jnp.float32)
     key_all = jnp.dot(stacked, pieces[1], preferred_element_type=jnp.float32)

time: 878 us -> 800 us (0.911)
  waiting for transfers between devices: 741 us -> 600 us
  blocking collectives: 63.2 us -> 99.9 us
  local copies, waits for them, and re-layouts: 5.08 us -> 30.7 us
    all_gather x1 -> x0, waiting for transfers between devices: 78.3 us -> none  [on_device(): lax.all_gather(w_value, 'seq', axis=0, tiled=True)]
    all_gather x1, waiting for transfers between devices: 80.4 us -> 42.5 us  [on_device(): lax.all_gather(w_query, 'seq', axis=0, tiled=True)]
    all_to_all x0 -> x1, blocking collectives: none -> 36.7 us  [gather_by_exchange(): return lax.all_to_all(copies, axis, dim, dim, tiled=True)]
    unnamed x10 -> x77, local copies, waits for them, and re-layouts: 3.41 us -> 29 us
    all_gather x1, waiting for transfers between devices: 80.6 us -> 66 us  [on_device(): lax.all_gather(w_key, 'seq', axis=0, tiled=True)]
    all_gather x1, waiting for transfers between devices: 10.3 us -> 0.01 us  [on_device(): lax.all_gather(scaled(stream_wide, stream_sq, gain_slice), 'head', axis=1...]
  transfers between devices with their start and end apart: 11 -> 10, of which waited for: 11 -> 9; matrix products, arithmetic and copies ran while one was open for 6% -> 9% of each run, Pallas kernels for 0% -> 0%
where the time goes in v1:
time: 800 us; the launch traced here: 797 us
  waiting for transfers between devices  600 us (75%)
  blocking collectives  99.9 us (12%)
  matrix products  39.6 us (5%)
  local copies, waits for them, and re-layouts  30.7 us (4%)
  between operations  14.5 us (2%)
  other arithmetic  12.1 us (2%)
    all_gather x1, waiting for transfers between devices, on_device(): lax.all_gather(w_out, 'seq', axis=1, tiled=True)  80 us
    all_gather x1, waiting for transfers between devices, on_device(): lax.all_gather(cache_k, 'seq', axis=0, tiled=True)  79.5 us
    all_gather x1, waiting for transfers between devices, on_device(): lax.all_gather(rot_key, 'seq', axis=0, tiled=True)  78 us
    all_gather x1, waiting for transfers between devices, on_device(): lax.all_gather(cache_v, 'seq', axis=0, tiled=True)  73.1 us
    all_gather x1, waiting for transfers between devices, on_device(): lax.all_gather(values_new, 'seq', axis=0, tiled=True)  72.4 us
    all_gather x1, waiting for transfers between devices, on_device(): lax.all_gather(w_key, 'seq', axis=0, tiled=True)  66 us
    all_gather x1, waiting for transfers between devices, on_device(): rows_piece = lax.all_gather(picture_rows, 'seq', axis=0, tiled=True)  64.4 us
    all_gather x1, waiting for transfers between devices, on_device(): lax.all_gather(w_query, 'seq', axis=0, tiled=True)  42.5 us
  transfers between devices with their start and end apart: 10, of which 9 were waited for; matrix products, arithmetic and copies ran while one was open for 9% of the time, Pallas kernels for 0%

profile of v1, /device:TPU:2, one launch (start us, length us, event | category | flops | bytes accessed | tf_op | source)
XLA Modules:
  0.0 797.1 jit_solution(15894686588040318782)
XLA Ops:
  7.3 1.3 dynamic-slice
  9.2 0.8 dynamic_slice.3
  10.0 0.8 dynamic-update-slice
  10.8 20.5 %all-reduce = s32[2048]{0:T(1024)S(1)} all-reduce(s32[2048]{0:T(1024)S(1)} %dynamic-update-slice), channel_id=1, replica_groups=mesh['seq'=64,'head'=8] {'seq'}, use_global_device_ids=true, to_apply=%add | all-reduce | flops 2048 | bytes 16384
  31.4 0.8 fusion.60
  32.5 64.4 %all-gather.10.cloned.1.call-done = bf16[2048,512]{1,0:T(8,128)(2,1)} async-done(((bf16[32,512]{1,0:T(8,128)(2,1)}), bf16[2048,512]{1,0:T(8,128)(2,1)}) %all-gather.10.cloned.1.call-update) | async-done | bytes 2097168 | tf_op jit(solution)/shard_map/all_gather | solution.py:79
  96.8 2.2 multiply_reduce_fusion.1
  99.0 18.1 %all-reduce.1 = (f32[128]{0:T(128)S(1)}, f32[8]{0:T(128)S(1)}) all-reduce(f32[128]{0:T(128)S(1)} %get-tuple-element.24, f32[8]{0:T(128)S(1)} %fusion.60), channel_id=1, replica_groups=mesh['seq'=64,'head'=8] {'head'}, use_global_device_ids=true, to_apply=%region_2.3 | all-reduce | flops 136 | bytes 1088 | tf_op jit(solution)/shard_map/psum | solution.py:94
  117.1 0.8 multiply_convert_fusion
  120.0 0.7 constant_dynamic-update-slice_fusion.64
  120.7 0.7 constant_dynamic-update-slice_fusion.63
  121.4 0.7 constant_dynamic-update-slice_fusion.62
  122.2 0.7 constant_dynamic-update-slice_fusion.61
  122.9 0.7 constant_dynamic-update-slice_fusion.60
  123.6 0.7 constant_dynamic-update-slice_fusion.59
  124.3 0.7 constant_dynamic-update-slice_fusion.58
  125.1 0.7 constant_dynamic-update-slice_fusion.57
  125.8 0.7 constant_dynamic-update-slice_fusion.56
  126.5 0.7 constant_dynamic-update-slice_fusion.55
  127.2 0.7 constant_dynamic-update-slice_fusion.54
  128.0 0.7 constant_dynamic-update-slice_fusion.53
  128.7 0.7 constant_dynamic-update-slice_fusion.52
  129.4 0.7 constant_dynamic-update-slice_fusion.51
  130.1 0.7 constant_dynamic-update-slice_fusion.50
  130.9 0.7 constant_dynamic-update-slice_fusion.49
  131.6 0.7 constant_dynamic-update-slice_fusion.48
  132.3 0.7 constant_dynamic-update-slice_fusion.47
  133.0 0.7 constant_dynamic-update-slice_fusion.46
  133.8 0.7 constant_dynamic-update-slice_fusion.45
  134.5 0.7 constant_dynamic-update-slice_fusion.44
  135.2 0.7 constant_dynamic-update-slice_fusion.43
  135.9 0.7 constant_dynamic-update-slice_fusion.42
  136.7 0.7 constant_dynamic-update-slice_fusion.41
  137.4 0.7 constant_dynamic-update-slice_fusion.40
  138.1 0.7 constant_dynamic-update-slice_fusion.39
  139.6 0.7 constant_dynamic-update-slice_fusion.37
  140.3 0.7 constant_dynamic-update-slice_fusion.36
  141.0 0.7 constant_dynamic-update-slice_fusion.35
  141.7 0.7 constant_dynamic-update-slice_fusion.34
  143.9 0.7 constant_dynamic-update-slice_fusion.31
  144.6 0.7 fusion.89
  145.5 0.8 fusion.62
  146.2 24.6 %all_gather.36 = bf16[8,4096]{1,0:T(8,128)(2,1)S(1)} all-gather(bf16[8,512]{1,0:T(8,128)(2,1)S(1)} %fusion.62), channel_id=1, replica_groups=mesh['seq'=64,'head'=8] {'head'}, dimensions={1}, use_global_device_ids=true | all-gather | bytes 73728 | tf_op jit(solution)/shard_map/all_gather | solution.py:99
  170.8 1.3 constant_dynamic-update-slice_fusion.1
  172.1 66.0 %all-gather.16.cloned.1.call-done = bf16[4096,128]{1,0:T(8,128)(2,1)} async-done(((bf16[64,128]{1,0:T(8,128)(2,1)}), bf16[4096,128]{1,0:T(8,128)(2,1)}) %all-gather.16.cloned.1.call-update) | async-done | bytes 1048592 | tf_op jit(solution)/shard_map/all_gather | solution.py:106
  238.2 1.7 fusion.90
  240.0 0.9 fusion.33
  242.4 36.7 %all_to_all.12 = bf16[64,64,128]{2,1,0:T(8,128)(2,1)S(1)} all-to-all(bf16[64,64,128]{2,1,0:T(8,128)(2,1)S(1)} %bitcast.59), channel_id=1, replica_groups=mesh['seq'=64,'head'=8] {'seq'}, dimensions={0} | all-to-all | bytes 2097152 | tf_op jit(solution)/shard_map/all_to_all | solution.py:15
  280.3 0.9 fusion.34
  282.9 42.5 %all-gather.14.cloned.1.call-done = bf16[4096,512]{1,0:T(8,128)(2,1)} async-done(((bf16[64,512]{1,0:T(8,128)(2,1)}), bf16[4096,512]{1,0:T(8,128)(2,1)}) %all-gather.14.cloned.1.call-update) | async-done | bytes 4194320 | tf_op jit(solution)/shard_map/all_gather | solution.py:105
  325.4 2.9 fusion.41
  328.7 79.5 %all-gather.18.cloned.1.call-done = bf16[4096,128]{1,0:T(8,128)(2,1)} async-done(((bf16[64,128]{1,0:T(8,128)(2,1)}), bf16[4096,128]{1,0:T(8,128)(2,1)}) %all-gather.18.cloned.1.call-update) | async-done | bytes 1048592 | tf_op jit(solution)/shard_map/all_gather | solution.py:152
  408.2 5.7 multiply_reduce_fusion
  413.9 78.0 %all-gather.22.cloned.1.call-done = bf16[8192,128]{1,0:T(8,128)(2,1)} async-done(((bf16[128,128]{1,0:T(8,128)(2,1)}), bf16[8192,128]{1,0:T(8,128)(2,1)}) %all-gather.22.cloned.1.call-update) | async-done | bytes 2097168 | tf_op jit(solution)/shard_map/all_gather | solution.py:158
  492.0 5.0 fusion
  497.0 1.5 fusion.6
  498.5 5.0 fusion.1
  503.5 72.4 %all-gather.24.cloned.1.call-done = bf16[8192,128]{1,0:T(8,128)(2,1)} async-done(((bf16[128,128]{1,0:T(8,128)(2,1)}), bf16[8192,128]{1,0:T(8,128)(2,1)}) %all-gather.24.cloned.1.call-update) | async-done | bytes 2097168 | tf_op jit(solution)/shard_map/all_gather | solution.py:159
  575.9 9.9 %fusion.3 = f32[4,128,128]{1,2,0:T(8,128)S(1)} fusion(f32[4,128,8192]{2,1,0:T(8,128)} %copy-done, f32[4,128]{1,0:T(4,128)S(1)} %get-tuple-element.18, pred[128,8192]{1,0:T(8,128)(4,1)S(1)} %iota_compare_fusion, bf16[8192,128]{1,0:T(8,128)(2,1)} %all-gather.24.cloned.1.call-done), kind=kOutput, calls=%fused_computation.6 | convolution fusion | flops 1094713344 | bytes 20187136 | tf_op jit(solution)/shard_map/kgtn,nkd->kgtd/dot_general | solution.py:51
  585.8 73.1 %all-gather.20.cloned.1.call-done = bf16[4096,128]{1,0:T(8,128)(2,1)} async-done(((bf16[64,128]{1,0:T(8,128)(2,1)}), bf16[4096,128]{1,0:T(8,128)(2,1)}) %all-gather.20.cloned.1.call-update) | async-done | bytes 1048592 | tf_op jit(solution)/shard_map/all_gather | solution.py:153
  658.9 5.4 fusion.38
  664.3 80.0 %all-gather.26.cloned.1.call-done = bf16[512,4096]{0,1:T(8,128)(2,1)} async-done(((bf16[512,64]{0,1:T(8,128)(2,1)}), bf16[512,4096]{0,1:T(8,128)(2,1)}) %all-gather.26.cloned.1.call-update) | async-done | bytes 4194320 | tf_op jit(solution)/shard_map/all_gather | solution.py:171
  744.3 4.7 convolution_convert_fusion
  749.0 41.2 %reduce-scatter.2.cloned.1.call-done = bf16[128,512]{1,0:T(8,128)(2,1)} async-done(((bf16[128,4096]{1,0:T(8,128)(2,1)}), bf16[128,512]{1,0:T(8,128)(2,1)}) %reduce-scatter.2.cloned.1.call-update) | async-done | bytes 131088 | tf_op jit(solution)/shard_map/reduce_scatter | solution.py:174
  (88 shorter events, 10.2 us)
Async XLA Ops:
  6.5 234.4 %copy-start.2 = (bf16[64,128]{1,0:T(8,128)(2,1)S(1)}, bf16[64,128]{1,0:T(8,128)(2,1)}, u32[]{:S(2)}) copy-start(bf16[64,128]{1,0:T(8,128)(2,1)} %param.18) | copy-start | bytes 49156
  6.5 233.4 %copy-start.3 = (bf16[64,128]{1,0:T(8,128)(2,1)S(1)}, bf16[64,128]{1,0:T(8,128)(2,1)}, u32[]{:S(2)}) copy-start(bf16[64,128]{1,0:T(8,128)(2,1)} %param.20) | copy-start | bytes 49156
  6.5 273.7 %copy-start.4 = (bf16[64,128]{1,0:T(8,128)(2,1)S(1)}, bf16[64,128]{1,0:T(8,128)(2,1)}, u32[]{:S(2)}) copy-start(bf16[64,128]{1,0:T(8,128)(2,1)} %param.21) | copy-start | bytes 49156
  6.5 90.3 %all-gather.10.cloned.1.call-start = ((), (), s32[]{:S(2)}) async-start(), calls=%async_computation.2 | async-start | bytes 2129920 | tf_op jit(solution)/shard_map/all_gather | solution.py:79
  7.3 163.5 %all-gather.12.cloned.1.call-start = ((), (), s32[]{:S(2)}) async-start(), calls=%async_computation.3 | async-start | bytes 1179648 | tf_op jit(solution)/shard_map/all_gather | solution.py:98
  117.9 120.3 %all-gather.16.cloned.1.call-start = ((), (), s32[]{:S(2)}) async-start(), calls=%async_computation.5 | async-start | bytes 1064960 | tf_op jit(solution)/shard_map/all_gather | solution.py:106
  118.6 206.8 %all-gather.14.cloned.1.call-start = ((), (), s32[]{:S(2)}) async-start(), calls=%async_computation.4 | async-start | bytes 4259840 | tf_op jit(solution)/shard_map/all_gather | solution.py:105
  119.2 289.0 %all-gather.18.cloned.1.call-start = ((), (), s32[]{:S(2)}) async-start(), calls=%async_computation.6 | async-start | bytes 1064960 | tf_op jit(solution)/shard_map/all_gather | solution.py:152
  240.9 251.1 %all-gather.22.cloned.1.call-start = ((), (), s32[]{:S(2)}) async-start(), calls=%async_computation.8 | async-start | bytes 2129920 | tf_op jit(solution)/shard_map/all_gather | solution.py:158
  242.2 333.7 %all-gather.24.cloned.1.call-start = ((), (), s32[]{:S(2)}) async-start(), calls=%async_computation.9 | async-start | bytes 2129920 | tf_op jit(solution)/shard_map/all_gather | solution.py:159
  280.2 378.7 %all-gather.20.cloned.1.call-start = ((), (), s32[]{:S(2)}) async-start(), calls=%async_computation.7 | async-start | bytes 1064960 | tf_op jit(solution)/shard_map/all_gather | solution.py:153
  281.2 463.1 %all-gather.26.cloned.1.call-start = ((), (), s32[]{:S(2)}) async-start(), calls=%async_computation.10 | async-start | bytes 4259840 | tf_op jit(solution)/shard_map/all_gather | solution.py:171
  281.9 508.3 %reduce-scatter.2.cloned.1.call-start = ((), (), s32[]{:S(2)}) async-start(), calls=%async_computation.11 | async-start | bytes 1179648 | tf_op jit(solution)/shard_map/reduce_scatter | solution.py:174
  492.0 5.0 copy-start.1
  496.9 6.5 copy-start
Sparse Core Ops, SparseCore 0:
  10.7 86.0 all-gather.9
  118.0 38.0 all-gather.11
  159.5 78.6 all-gather.15
  241.4 84.0 all-gather.13
  328.6 79.4 all-gather.17
  411.4 80.5 all-gather.21
  495.3 80.5 all-gather.23
  579.2 79.6 all-gather.19
  662.3 82.0 all-gather.25
  749.1 41.0 reduce-scatter.1
